TPU v7x, 128 devices: a whole 4x4x4 slice. The times are simulated.
128 devices in a mesh: row: 8 (over z, y_lo), col: 16 (over x, y_hi, core).
Axes of the slice: x: 4, y: 4 (y_hi: 2, y_lo: 2; y = y_hi * 2 + y_lo), z: 4, core: 2. Of those that a mesh axis runs over, the one named last changes fastest.
Arguments:
- t2_amps: bfloat16 [16384, 2048], P('row', 'col'), may hold values from -6 to 6
- v_ints: bfloat16 [2048, 32768], P('row', 'col'), may hold values from -0.125 to 0.125
- t2_mask: int32 [128, 16], P('row', 'col'), may hold values 0 or 1
- v_mask: int32 [16, 256], P('row', 'col'), may hold values 0 or 1
Outputs:
- ladder: bfloat16 [16384, 32768], P('row', 'col')
All inputs are finite; a program needn't handle non-finite values. No bound on the sum of `t2_mask` or of `v_mask` on one device may be relied on, other than what follows from the above.
Results may differ from a plain program's by a relative error of at most 0.001.
Values may be sent and summed in bfloat16 or wider, within the bound.
A program may use at most 64 MiB of HBM per device.

v0:
```python
import jax
import jax.numpy as jnp
from jax import lax
from jax.sharding import PartitionSpec as P

TILE = 128


def expand(mask, rows, cols):
    kept = jnp.broadcast_to(mask[:, None, :, None] > 0, (mask.shape[0], TILE, mask.shape[1], TILE))
    return kept.reshape(rows, cols)


def body(t2_amps, v_ints, t2_mask, v_mask):
    masked_t2 = jnp.where(
        expand(t2_mask, t2_amps.shape[0], t2_amps.shape[1]), t2_amps, jnp.zeros_like(t2_amps)
    )
    masked_v = jnp.where(
        expand(v_mask, v_ints.shape[0], v_ints.shape[1]), v_ints, jnp.zeros_like(v_ints)
    )
    amp_whole = lax.all_gather(masked_t2, "col", axis=1, tiled=True)
    result = jnp.dot(
        amp_whole,
        lax.all_gather(masked_v, "row", axis=0, tiled=True),
        preferred_element_type=jnp.float32,
    )
    return result.astype(jnp.bfloat16)


def solution(mesh):
    in_specs = (P("row", "col"), P("row", "col"), P("row", "col"), P("row", "col"))
    out_specs = P("row", "col")
    return jax.shard_map(body, mesh=mesh, in_specs=in_specs, out_specs=out_specs, check_vma=False)
```

profile of v0, /device:TPU:1, one launch (start us, length us, event | category | flops | bytes accessed | tf_op | source)
XLA Modules:
  0.0 295.8 jit_solution(9353750892337013907)
XLA Ops:
  6.5 0.0 all-gather.5.cloned.1.call-start
  6.5 0.7 broadcast_compare_fusion
  7.2 0.2 broadcast_in_dim.26
  7.4 2.5 bitcast_select_fusion
  9.9 0.0 all-gather.5.cloned.1.call-update
  9.9 0.0 all-gather.3.cloned.1.call-start
  10.0 0.7 compare_bitcast_fusion
  10.6 0.1 broadcast_bitcast_fusion
  10.7 2.2 broadcast_select_fusion
  12.9 0.0 all-gather.3.cloned.1.call-update
  12.9 168.7 %all-gather.5.cloned.1.call-done = bf16[2048,2048]{1,0:T(8,128)(2,1)} async-done(((bf16[256,2048]{1,0:T(8,128)(2,1)}), bf16[2048,2048]{1,0:T(8,128)(2,1)}) %all-gather.5.cloned.1.call-update) | async-done | bytes 8388624 | tf_op jit(solution)/shard_map/all_gather | solution.py:24
  181.6 83.9 %all-gather.3.cloned.1.call-done = bf16[2048,2048]{1,0:T(8,128)(2,1)} async-done(((bf16[2048,128]{1,0:T(8,128)(2,1)}), bf16[2048,2048]{1,0:T(8,128)(2,1)}) %all-gather.3.cloned.1.call-update) | async-done | bytes 8388624 | tf_op jit(solution)/shard_map/all_gather | solution.py:21
  265.5 23.5 %convolution_convert_fusion = bf16[2048,2048]{1,0:T(8,128)(2,1)} fusion(bf16[2048,2048]{1,0:T(8,128)(2,1)} %all-gather.3.cloned.1.call-done, bf16[2048,2048]{1,0:T(8,128)(2,1)} %all-gather.5.cloned.1.call-done), kind=kOutput, calls=%fused_computation | convolution fusion | flops 17184063488 | bytes 25165824 | tf_op jit(solution)/shard_map/dot_general | solution.py:22
Async XLA Ops:
  6.5 175.1 %all-gather.5.cloned.1.call-start = ((), (), s32[]{:S(2)}) async-start(), calls=%async_computation.1 | async-start | bytes 9437184 | tf_op jit(solution)/shard_map/all_gather | solution.py:24
  9.9 255.6 %all-gather.3.cloned.1.call-start = ((), (), s32[]{:S(2)}) async-start(), calls=%async_computation | async-start | bytes 8912896 | tf_op jit(solution)/shard_map/all_gather | solution.py:21
Sparse Core Ops, SparseCore 0:
  10.0 171.5 all-gather.4
  183.9 81.5 all-gather.2
where the time goes:
time: 296 us
  waiting for transfers between devices  253 us (85%)
  matrix products  23.5 us (8%)
  between operations  13.4 us (5%)
  other arithmetic  5.99 us (2%)
    all_gather x1, waiting for transfers between devices, body(): lax.all_gather(masked_v, 'row', axis=0, tiled=True)  169 us
    all_gather x1, waiting for transfers between devices, body(): amp_whole = lax.all_gather(masked_t2, 'col', axis=1, tiled=True)  83.9 us
    dot_general x1, matrix products, body(): jnp.dot(amp_whole, lax.all_gather(masked_v, 'row', axis=0, tiled=True), p...  23.5 us
  transfers between devices with their start and end apart: 2, of which 2 were waited for; matrix products, arithmetic and copies ran while one was open for 1% of the time, Pallas kernels for 0%

commit v1 on v0

--- a/solution.py
+++ b/solution.py
@@ -21,7 +21,9 @@
     amp_whole = lax.all_gather(masked_t2, "col", axis=1, tiled=True)
     result = jnp.dot(
         amp_whole,
-        lax.all_gather(masked_v, "row", axis=0, tiled=True),
+        jnp.concatenate(
+            lax.all_to_all(jnp.stack([masked_v] * lax.axis_size("row")), "row", 0, 0), axis=0
+        ),
         preferred_element_type=jnp.float32,
     )
     return result.astype(jnp.bfloat16)

time: 296 us -> 173 us (0.58)
  waiting for transfers between devices: 253 us -> 0.02 us
  blocking collectives: 0 us -> 129 us
    all_gather x1 -> x0, waiting for transfers between devices: 169 us -> none  [body(): lax.all_gather(masked_v, 'row', axis=0, tiled=True)]
    all_to_all x0 -> x1, blocking collectives: none -> 129 us  [body(): lax.all_to_all(jnp.stack([masked_v] * lax.axis_size('row')), 'row', 0, 0)]
    all_gather x1, waiting for transfers between devices: 83.9 us -> 0.01 us  [body(): amp_whole = lax.all_gather(masked_t2, 'col', axis=1, tiled=True)]
  transfers between devices with their start and end apart: 2 -> 1, of which waited for: 2 -> 0; matrix products, arithmetic and copies ran while one was open for 1% -> 2% of each run, Pallas kernels for 0% -> 0%
where the time goes in v1:
time: 173 us; the launch traced here: 172 us
  blocking collectives  129 us (75%)
  matrix products  23.5 us (14%)
  between operations  13.4 us (8%)
  other arithmetic  5.02 us (3%)
    all_to_all x1, blocking collectives, body(): lax.all_to_all(jnp.stack([masked_v] * lax.axis_size('row')), 'row', 0, 0)  129 us
    dot_general x1, matrix products, body(): jnp.dot(amp_whole, jnp.concatenate(lax.all_to_all(jnp.stack([masked_v] *...  23.5 us
  transfers between devices with their start and end apart: 1, of which 0 were waited for; matrix products, arithmetic and copies ran while one was open for 2% of the time, Pallas kernels for 0%

profile of v1, /device:TPU:1, one launch (start us, length us, event | category | flops | bytes accessed | tf_op | source)
XLA Modules:
  0.0 171.9 jit_solution(8047747743320157334)
XLA Ops:
  6.5 0.0 all-gather.2.cloned.1.call-start
  6.5 0.7 compare_bitcast_fusion
  7.2 0.1 broadcast_bitcast_fusion
  7.3 2.2 %broadcast_select_fusion = bf16[2048,128]{1,0:T(8,128)(2,1)} fusion(bf16[2048,128]{1,0:T(8,128)(2,1)} %param.4, pred[2048]{0:T(1024)(128)(4,1)S(1)} %broadcast_bitcast_fusion), kind=kLoop, calls=%fused_computation.2 | loop fusion | flops 262144 | bytes 1050624 | tf_op jit(solution)/shard_map/jit(_where)/select_n | solution.py:15
  9.4 0.0 all-gather.2.cloned.1.call-update
  9.5 0.7 broadcast_compare_fusion
  10.2 0.2 broadcast_in_dim.26
  10.4 1.5 bitcast_select_fusion
  11.9 1.1 stack.2
  12.9 128.6 %all_to_all.5 = bf16[8,256,2048]{2,1,0:T(8,128)(2,1)} all-to-all(bf16[8,256,2048]{2,1,0:T(8,128)(2,1)S(1)} %stack.2), channel_id=1, replica_groups=mesh['row'=8,'col'=16] {'row'}, dimensions={0} | all-to-all | bytes 16777216 | tf_op jit(solution)/shard_map/all_to_all | solution.py:25
  141.6 0.0 all-gather.2.cloned.1.call-done
  141.6 23.5 %convolution_convert_fusion = bf16[2048,2048]{1,0:T(8,128)(2,1)} fusion(bf16[2048,2048]{1,0:T(8,128)(2,1)} %all-gather.2.cloned.1.call-done, bf16[2048,2048]{1,0:T(8,128)(2,1)} %bitcast.11), kind=kOutput, calls=%fused_computation | convolution fusion | flops 17184063488 | bytes 25165824 | tf_op jit(solution)/shard_map/dot_general | solution.py:22
Async XLA Ops:
  6.5 135.0 %all-gather.2.cloned.1.call-start = ((), (), s32[]{:S(2)}) async-start(), calls=%async_computation.1 | async-start | bytes 8912896 | tf_op jit(solution)/shard_map/all_gather | solution.py:21
Sparse Core Ops, SparseCore 0:
  9.6 110.2 all-gather.1
